TPU v7x, 256 devices: a whole 4x4x8 slice. The times are simulated.
256 devices in a mesh: pipe: 8 (over z), dp: 4 (over y), expert: 8 (over x, core).
Axes of the slice: x: 4, y: 4, z: 8, core: 2. Of those that a mesh axis runs over, the one named last changes fastest.
Arguments:
- tokens: bfloat16 [4096, 4096], P(('dp', 'expert'), 'pipe'), may hold values from -6 to 6
- routes: int32 [4096, 6], P(('dp', 'expert')), may hold values from 0 to 31, all different within a row; in each aligned block of 128 rows (0 to 127, 128 to 255, ...) at most 32 rows name the same one
- gates: float32 [4096, 6], P(('dp', 'expert')), may hold values from 0.1 to 0.5
- w_gate: bfloat16 [32, 4096, 1024], P(('dp', 'expert'), 'pipe'), may hold values from -0.09375 to 0.09375
- w_up: bfloat16 [32, 4096, 1024], P(('dp', 'expert'), 'pipe'), may hold values from -0.09375 to 0.09375
- w_down: bfloat16 [32, 1024, 4096], P(('dp', 'expert'), None, 'pipe'), may hold values from -0.1875 to 0.1875
- grad_out: bfloat16 [4096, 4096], P(('dp', 'expert'), 'pipe'), may hold values from -6 to 6
Outputs:
- mixed: bfloat16 [4096, 4096], P(('dp', 'expert'), 'pipe')
- grad_tokens: bfloat16 [4096, 4096], P(('dp', 'expert'), 'pipe')
- grad_gate: bfloat16 [32, 4096, 1024], P(('dp', 'expert'), 'pipe')
- grad_up: bfloat16 [32, 4096, 1024], P(('dp', 'expert'), 'pipe')
- grad_down: bfloat16 [32, 1024, 4096], P(('dp', 'expert'), None, 'pipe')
Inputs may be any that keep to these rules, and one draw needn't show every extreme that they name: `routes`: each row names 6 different experts; in each aligned block of 128 rows no expert is named by more than 32 rows, a bound that some block reaches.
All inputs are finite; a program needn't handle non-finite values.
Results may differ from a plain program's by a relative error of at most 0.0065.
Values may be sent and summed in bfloat16 or wider, within the bound.
A program may use at most 128 MiB of HBM per device.

v0:
```python
import jax
import jax.numpy as jnp
from jax import lax
from jax.sharding import PartitionSpec as P

CAP = 32


def slot_layout(routes, num_experts):
    tok_count, top_count = routes.shape
    chosen = routes.reshape(tok_count * top_count)
    expert_ids = jnp.arange(num_experts, dtype=jnp.int32)
    onehot = (chosen[:, None] == expert_ids[None, :]).astype(jnp.int32)
    earlier = jnp.cumsum(onehot, axis=0) - onehot
    position = jnp.sum(earlier * onehot, axis=1)
    target = chosen * CAP + position
    slot_ids = jnp.arange(num_experts * CAP, dtype=jnp.int32)
    placed = slot_ids[:, None] == target[None, :]
    return placed.reshape(num_experts * CAP, tok_count, top_count)


def local(tokens, routes, gates, w_gate, w_up, w_down, grad_out):
    groups = lax.axis_size(("dp", "expert"))
    local_experts = w_gate.shape[0]
    num_experts = local_experts * groups
    slice_width = tokens.shape[1]
    placed = slot_layout(routes, num_experts)
    dispatch = jnp.sum(placed.astype(jnp.int32), axis=2).astype(jnp.bfloat16)
    mixing = jnp.sum(jnp.where(placed, gates[None, :, :], 0.0), axis=2)
    outbound = jnp.dot(dispatch, tokens, preferred_element_type=jnp.float32).astype(jnp.bfloat16)
    outbound = outbound.reshape(num_experts, CAP, slice_width)
    scaled_out = jnp.dot(
        mixing, grad_out.astype(jnp.float32), precision=lax.Precision.HIGHEST
    ).astype(jnp.bfloat16)
    scaled_out = scaled_out.reshape(num_experts, CAP, slice_width)
    arrived, arrived_grad = (
        lax.all_to_all(outbound, ("dp", "expert"), split_axis=0, concat_axis=0, tiled=True),
        lax.all_to_all(scaled_out, ("dp", "expert"), split_axis=0, concat_axis=0, tiled=True),
    )
    expert_rows = arrived.reshape(groups, local_experts, CAP, slice_width)
    scaled = arrived_grad.reshape(groups, local_experts, CAP, slice_width)
    gate_part = jnp.einsum(
        "sjcd,jdf->sjcf", expert_rows, w_gate, preferred_element_type=jnp.float32
    )
    up_part = jnp.einsum("sjcd,jdf->sjcf", expert_rows, w_up, preferred_element_type=jnp.float32)
    gate_share, up_share = (
        lax.psum_scatter(gate_part, "pipe", scatter_dimension=3, tiled=True),
        lax.psum_scatter(up_part, "pipe", scatter_dimension=3, tiled=True),
    )
    hidden_share = (jax.nn.silu(gate_share) * up_share).astype(jnp.bfloat16)
    hidden = lax.all_gather(hidden_share, "pipe", axis=3, tiled=True)
    expert_out = jnp.einsum(
        "sjcf,jfd->sjcd", hidden, w_down, preferred_element_type=jnp.float32
    ).astype(jnp.bfloat16)
    returned = lax.all_to_all(
        expert_out.reshape(num_experts, CAP, slice_width),
        ("dp", "expert"),
        split_axis=0,
        concat_axis=0,
        tiled=True,
    )
    returned_rows = returned.reshape(num_experts * CAP, slice_width).astype(jnp.float32)
    mixed = jnp.dot(mixing.T, returned_rows, precision=lax.Precision.HIGHEST).astype(jnp.bfloat16)
    d_hidden_part = jnp.einsum("sjcd,jfd->sjcf", scaled, w_down, preferred_element_type=jnp.float32)
    d_hidden = lax.psum_scatter(d_hidden_part, "pipe", scatter_dimension=3, tiled=True)
    sig_gate = jax.nn.sigmoid(gate_share)
    d_gate_share = (d_hidden * up_share * sig_gate * (1.0 + gate_share * (1.0 - sig_gate))).astype(
        jnp.bfloat16
    )
    d_up_share = (d_hidden * gate_share * sig_gate).astype(jnp.bfloat16)
    d_gate, d_up = (
        lax.all_gather(d_gate_share, "pipe", axis=3, tiled=True),
        lax.all_gather(d_up_share, "pipe", axis=3, tiled=True),
    )
    d_rows = (
        jnp.einsum("sjcf,jdf->sjcd", d_gate, w_gate, preferred_element_type=jnp.float32)
        + jnp.einsum("sjcf,jdf->sjcd", d_up, w_up, preferred_element_type=jnp.float32)
    ).astype(jnp.bfloat16)
    back_rows = lax.all_to_all(
        d_rows.reshape(num_experts, CAP, slice_width),
        ("dp", "expert"),
        split_axis=0,
        concat_axis=0,
        tiled=True,
    )
    grad_tokens = jnp.dot(
        dispatch.T,
        back_rows.reshape(num_experts * CAP, slice_width),
        preferred_element_type=jnp.float32,
    ).astype(jnp.bfloat16)
    grad_gate = jnp.einsum(
        "sjcd,sjcf->jdf", expert_rows, d_gate, preferred_element_type=jnp.float32
    ).astype(jnp.bfloat16)
    grad_up = jnp.einsum(
        "sjcd,sjcf->jdf", expert_rows, d_up, preferred_element_type=jnp.float32
    ).astype(jnp.bfloat16)
    grad_down = jnp.einsum(
        "sjcf,sjcd->jfd", hidden, scaled, preferred_element_type=jnp.float32
    ).astype(jnp.bfloat16)
    return (mixed, grad_tokens, grad_gate, grad_up, grad_down)


def solution(mesh):
    placed = (
        P(("dp", "expert"), "pipe"),
        P(("dp", "expert"), None),
        P(("dp", "expert"), None),
        P(("dp", "expert"), "pipe", None),
        P(("dp", "expert"), "pipe", None),
        P(("dp", "expert"), None, "pipe"),
        P(("dp", "expert"), "pipe"),
    )
    return jax.shard_map(
        local,
        mesh=mesh,
        in_specs=placed,
        out_specs=(
            P(("dp", "expert"), "pipe"),
            P(("dp", "expert"), "pipe"),
            P(("dp", "expert"), "pipe", None),
            P(("dp", "expert"), "pipe", None),
            P(("dp", "expert"), None, "pipe"),
        ),
        check_vma=False,
    )
```

profile of v0, /device:TPU:1, one launch (start us, length us, event | category | flops | bytes accessed | tf_op | source)
XLA Modules:
  0.0 395.4 jit_solution(5158708211324095132)
XLA Ops:
  7.2 0.0 copy-start
  7.2 0.0 reduce-scatter.6.cloned.1.call-start
  7.2 0.9 copy.38
  8.1 0.1 eq.44
  8.2 0.1 eq.40
  8.4 1.7 reduce-window.6
  10.1 0.3 slice_reduce_fusion
  10.4 0.1 fusion.42
  10.5 0.1 reduce_sum.30
  10.7 0.1 copy.41
  10.7 0.7 multiply_add_fusion
  11.5 0.4 convert_reduce_fusion
  11.8 1.3 convolution_convert_fusion
  13.2 25.4 %all_to_all.20 = bf16[32,32,512]{2,1,0:T(8,128)(2,1)S(1)} all-to-all(bf16[32,32,512]{2,1,0:T(8,128)(2,1)S(1)} %bitcast.121), channel_id=1, replica_groups=mesh['pipe'=8,'dp'=4,'expert'=8] {'dp','expert'}, dimensions={0} | all-to-all | bytes 2097152 | tf_op jit(solution)/shard_map/all_to_all | solution.py:37
  38.6 0.0 copy-done.4
  38.6 3.2 convolution_bitcast_fusion.1
  41.8 0.0 reduce-scatter.6.cloned.1.call-update
  41.8 0.0 reduce-scatter.4.cloned.1.call-start
  41.9 4.4 %convolution_bitcast_fusion.2 = f32[32,1,32,1024]{3,2,0,1:T(8,128)} fusion(bf16[32,32,512]{2,1,0:T(8,128)(2,1)S(1)} %all_to_all.20, bf16[1,512,1024]{2,1,0:T(8,128)(2,1)} %param.10), kind=kOutput, calls=%fused_computation.5 | convolution fusion | flops 1073741824 | bytes 6291456 | tf_op jit(solution)/shard_map/sjcd,jdf->sjcf/dot_general | solution.py:42
  46.3 0.0 copy-start.6
  46.3 0.0 copy-start.5
  46.3 0.0 reduce-scatter.4.cloned.1.call-update
  46.4 0.0 reduce-scatter.8.cloned.1.call-start
  46.4 0.6 copy-done.6
  47.0 0.4 select_reduce_fusion
  47.4 0.0 copy-done.5
  47.4 1.0 convolution_convert_fusion.1
  48.4 20.7 %all_to_all.21 = bf16[32,32,512]{2,1,0:T(8,128)(2,1)S(1)} all-to-all(bf16[32,32,512]{2,1,0:T(8,128)(2,1)S(1)} %bitcast.122), channel_id=1, replica_groups=mesh['pipe'=8,'dp'=4,'expert'=8] {'dp','expert'}, dimensions={0} | all-to-all | bytes 2097152 | tf_op jit(solution)/shard_map/all_to_all | solution.py:38
  69.1 0.0 copy-start.1
  69.1 1.0 copy-done.1
  70.0 0.0 copy-done
  70.0 3.2 convolution_bitcast_fusion
  73.3 0.0 reduce-scatter.8.cloned.1.call-update
  73.3 0.0 all-gather.4.cloned.1.call-start
  73.3 23.0 %reduce-scatter.6.cloned.1.call-done = f32[32,1,32,128]{3,2,0,1:T(8,128)} async-done(((f32[32,1,32,1024]{3,2,0,1:T(8,128)}), f32[32,1,32,128]{3,2,0,1:T(8,128)}) %reduce-scatter.6.cloned.1.call-update) | async-done | bytes 524304 | tf_op jit(solution)/shard_map/reduce_scatter | solution.py:48
  96.3 56.5 %reduce-scatter.4.cloned.1.call-done = f32[32,1,32,128]{3,2,0,1:T(8,128)} async-done(((f32[32,1,32,1024]{3,2,0,1:T(8,128)}), f32[32,1,32,128]{3,2,0,1:T(8,128)}) %reduce-scatter.4.cloned.1.call-update) | async-done | bytes 524304 | tf_op jit(solution)/shard_map/reduce_scatter | solution.py:47
  152.9 56.6 %reduce-scatter.8.cloned.1.call-done = f32[32,1,32,128]{3,2,0,1:T(8,128)} async-done(((f32[32,1,32,1024]{3,2,0,1:T(8,128)}), f32[32,1,32,128]{3,2,0,1:T(8,128)}) %reduce-scatter.8.cloned.1.call-update) | async-done | bytes 524304 | tf_op jit(solution)/shard_map/reduce_scatter | solution.py:65
  209.4 2.5 multiply_convert_fusion.1
  211.9 0.0 all-gather.4.cloned.1.call-update
  212.0 0.0 all-gather.8.cloned.1.call-start
  212.0 0.5 all-gather.8.cloned.1.call-update
  212.6 0.0 all-gather.6.cloned.1.call-start
  212.6 0.5 all-gather.6.cloned.1.call-update
  213.1 40.6 %all-gather.4.cloned.1.call-done = bf16[32,1,32,1024]{3,2,0,1:T(8,128)(2,1)} async-done(((bf16[32,1,32,128]{3,2,0,1:T(8,128)(2,1)}), bf16[32,1,32,1024]{3,2,0,1:T(8,128)(2,1)}) %all-gather.4.cloned.1.call-update) | async-done | bytes 2097168 | tf_op jit(solution)/shard_map/all_gather | solution.py:51
  253.7 3.8 fusion.20
  257.6 12.2 %all-to-all-start.1 = ((bf16[32,32,512]{2,1,0:T(8,128)(2,1)}), bf16[32,32,512]{2,1,0:T(8,128)(2,1)}, u32[]{:S(2)}, u32[]{:S(2)}) async-start(bf16[32,32,512]{2,1,0:T(8,128)(2,1)} %fusion.20), calls=%async_computation.3 | async-start | bytes 2097152 | tf_op jit(solution)/shard_map/all_to_all | solution.py:55
  269.8 31.9 %all-gather.8.cloned.1.call-done = bf16[32,1,32,1024]{3,2,0,1:T(8,128)(2,1)} async-done(((bf16[32,1,32,128]{3,2,0,1:T(8,128)(2,1)}), bf16[32,1,32,1024]{3,2,0,1:T(8,128)(2,1)}) %all-gather.8.cloned.1.call-update) | async-done | bytes 2097168 | tf_op jit(solution)/shard_map/all_gather | solution.py:73
  301.7 0.0 copy-start.2
  301.7 0.0 copy-start.7
  301.7 4.6 %fusion.2 = f32[32,32,512]{2,1,0:T(8,128)} fusion(bf16[32,1,32,1024]{3,2,0,1:T(8,128)(2,1)} %all-gather.8.cloned.1.call-done, bf16[1,512,1024]{2,1,0:T(8,128)(2,1)} %param.11), kind=kOutput, calls=%fused_computation.11 | convolution fusion | flops 1073741824 | bytes 5242880 | tf_op jit(solution)/shard_map/sjcf,jdf->sjcd/dot_general | solution.py:77
  306.3 0.0 copy-done.2
  306.3 0.0 copy-done.7
  306.3 2.3 fusion.29
  308.6 41.2 %all-gather.6.cloned.1.call-done = bf16[32,1,32,1024]{3,2,0,1:T(8,128)(2,1)} async-done(((bf16[32,1,32,128]{3,2,0,1:T(8,128)(2,1)}), bf16[32,1,32,1024]{3,2,0,1:T(8,128)(2,1)}) %all-gather.6.cloned.1.call-update) | async-done | bytes 2097168 | tf_op jit(solution)/shard_map/all_gather | solution.py:72
  349.8 0.0 copy-start.3
  349.8 5.0 %add_convert_fusion = bf16[32,32,512]{2,1,0:T(8,128)(2,1)} fusion(f32[32,32,512]{2,1,0:T(8,128)} %fusion.2, bf16[32,1,32,1024]{3,2,0,1:T(8,128)(2,1)} %all-gather.6.cloned.1.call-done, bf16[1,512,1024]{2,1,0:T(8,128)(2,1)} %param.10), kind=kOutput, calls=%fused_computation.21 | convolution fusion | flops 1074790400 | bytes 6291456 | tf_op jit(solution)/shard_map/sjcf,jdf->sjcd/dot_general | solution.py:76
  354.8 0.0 copy-done.3
  354.8 2.2 fusion.26
  357.0 0.0 all-to-all-done.1
  357.0 12.2 %all-to-all-start.3 = ((bf16[32,32,512]{2,1,0:T(8,128)(2,1)}), bf16[32,32,512]{2,1,0:T(8,128)(2,1)}, u32[]{:S(2)}, u32[]{:S(2)}) async-start(bf16[32,32,512]{2,1,0:T(8,128)(2,1)} %add_convert_fusion), calls=%async_computation.6 | async-start | bytes 2097152 | tf_op jit(solution)/shard_map/all_to_all | solution.py:79
  369.2 3.8 fusion.23
  373.1 2.6 convolution_convert_fusion.3
  375.6 10.7 %all-to-all-done.3 = bf16[32,32,512]{2,1,0:T(8,128)(2,1)} async-done(((bf16[32,32,512]{2,1,0:T(8,128)(2,1)}), bf16[32,32,512]{2,1,0:T(8,128)(2,1)}, u32[]{:S(2)}, u32[]{:S(2)}) %all-to-all-start.3) | async-done | bytes 1048608 | tf_op jit(solution)/shard_map/all_to_all | solution.py:79
  386.3 2.2 convolution_convert_fusion.2
  (3 shorter events, 0.0 us)
Async XLA Ops:
  7.2 62.9 %copy-start = (bf16[1,1024,512]{2,1,0:T(8,128)(2,1)S(1)}, bf16[1,1024,512]{2,1,0:T(8,128)(2,1)}, u32[]{:S(2)}) copy-start(bf16[1,1024,512]{2,1,0:T(8,128)(2,1)} %param.12) | copy-start | bytes 3145732
  7.2 89.1 %reduce-scatter.6.cloned.1.call-start = ((), (), s32[]{:S(2)}) async-start(), calls=%async_computation.8 | async-start | bytes 4718592 | tf_op jit(solution)/shard_map/reduce_scatter | solution.py:48
  11.5 27.1 %copy-start.4 = (bf16[1,512,1024]{2,1,0:T(8,128)(2,1)S(1)}, bf16[1,512,1024]{2,1,0:T(8,128)(2,1)}, u32[]{:S(2)}) copy-start(bf16[1,512,1024]{2,1,0:T(8,128)(2,1)} %param.11) | copy-start | bytes 3145732
  41.8 111.0 %reduce-scatter.4.cloned.1.call-start = ((), (), s32[]{:S(2)}) async-start(), calls=%async_computation.7 | async-start | bytes 4718592 | tf_op jit(solution)/shard_map/reduce_scatter | solution.py:47
  46.3 0.7 copy-start.6
  46.3 1.1 copy-start.5
  46.4 163.1 %reduce-scatter.8.cloned.1.call-start = ((), (), s32[]{:S(2)}) async-start(), calls=%async_computation.10 | async-start | bytes 4718592 | tf_op jit(solution)/shard_map/reduce_scatter | solution.py:65
  69.1 1.0 copy-start.1
  73.3 180.5 %all-gather.4.cloned.1.call-start = ((), (), s32[]{:S(2)}) async-start(), calls=%async_computation.9 | async-start | bytes 2359296 | tf_op jit(solution)/shard_map/all_gather | solution.py:51
  212.0 89.7 %all-gather.8.cloned.1.call-start = ((), (), s32[]{:S(2)}) async-start(), calls=%async_computation.12 | async-start | bytes 2359296 | tf_op jit(solution)/shard_map/all_gather | solution.py:73
  212.6 137.3 %all-gather.6.cloned.1.call-start = ((), (), s32[]{:S(2)}) async-start(), calls=%async_computation.11 | async-start | bytes 2359296 | tf_op jit(solution)/shard_map/all_gather | solution.py:72
  257.6 99.5 %all-to-all-start.1 = ((bf16[32,32,512]{2,1,0:T(8,128)(2,1)}), bf16[32,32,512]{2,1,0:T(8,128)(2,1)}, u32[]{:S(2)}, u32[]{:S(2)}) async-start(bf16[32,32,512]{2,1,0:T(8,128)(2,1)} %fusion.20), calls=%async_computation.3 | async-start | bytes 2097152 | tf_op jit(solution)/shard_map/all_to_all | solution.py:55
  301.7 4.6 %copy-start.2 = (bf16[32,32,512]{2,1,0:T(8,128)(2,1)S(1)}, bf16[32,32,512]{2,1,0:T(8,128)(2,1)}, u32[]{:S(2)}) copy-start(bf16[32,32,512]{2,1,0:T(8,128)(2,1)} %copy-done.1) | copy-start | bytes 3145732
  301.7 4.6 %copy-start.7 = (bf16[32,1,32,1024]{3,2,0,1:T(8,128)(2,1)S(1)}, bf16[32,1,32,1024]{3,2,0,1:T(8,128)(2,1)}, u32[]{:S(2)}) copy-start(bf16[32,1,32,1024]{3,2,0,1:T(8,128)(2,1)} %all-gather.4.cloned.1.call-done) | copy-start | bytes 6291460
  349.8 5.0 %copy-start.3 = (bf16[32,1,32,1024]{3,2,0,1:T(8,128)(2,1)S(1)}, bf16[32,1,32,1024]{3,2,0,1:T(8,128)(2,1)}, u32[]{:S(2)}) copy-start(bf16[32,1,32,1024]{3,2,0,1:T(8,128)(2,1)} %all-gather.8.cloned.1.call-done) | copy-start | bytes 6291460
  357.0 29.3 %all-to-all-start.3 = ((bf16[32,32,512]{2,1,0:T(8,128)(2,1)}), bf16[32,32,512]{2,1,0:T(8,128)(2,1)}, u32[]{:S(2)}, u32[]{:S(2)}) async-start(bf16[32,32,512]{2,1,0:T(8,128)(2,1)} %add_convert_fusion), calls=%async_computation.6 | async-start | bytes 2097152 | tf_op jit(solution)/shard_map/all_to_all | solution.py:79
Sparse Core Ops, SparseCore 0:
  42.0 54.3 reduce-scatter.5
  98.9 53.9 reduce-scatter.3
  155.4 53.9 reduce-scatter.7
  212.1 41.6 all-gather.3
  255.3 46.3 all-gather.7
  303.8 45.9 all-gather.5
where the time goes:
time: 396 us; the launch traced here: 395 us
  waiting for transfers between devices  262 us (66%)
  blocking collectives  46.1 us (12%)
  matrix products  39.7 us (10%)
  starting transfers between devices  24.7 us (6%)
  between operations  14.2 us (4%)
  other arithmetic  5.89 us (1%)
    reduce_scatter x1, waiting for transfers between devices, local(): lax.psum_scatter(d_hidden_part, 'pipe', scatter_dimension=3, tiled=True)  56.6 us
    reduce_scatter x1, waiting for transfers between devices, local(): lax.psum_scatter(gate_part, 'pipe', scatter_dimension=3, tiled=True)  56.5 us
    all_gather x1, waiting for transfers between devices, local(): lax.all_gather(d_gate_share, 'pipe', axis=3, tiled=True)  41.2 us
    all_gather x1, waiting for transfers between devices, local(): hidden = lax.all_gather(hidden_share, 'pipe', axis=3, tiled=True)  40.6 us
    all_gather x1, waiting for transfers between devices, local(): lax.all_gather(d_up_share, 'pipe', axis=3, tiled=True)  31.9 us
    all_to_all x1, blocking collectives, local(): lax.all_to_all(outbound, ('dp', 'expert'), split_axis=0, concat_axis=0, t...  25.4 us
    reduce_scatter x1, waiting for transfers between devices, local(): lax.psum_scatter(up_part, 'pipe', scatter_dimension=3, tiled=True)  23 us
    all_to_all x1, blocking collectives, local(): lax.all_to_all(scaled_out, ('dp', 'expert'), split_axis=0, concat_axis=0,...  20.7 us
  transfers between devices with their start and end apart: 8, of which 7 were waited for; matrix products, arithmetic and copies ran while one was open for 8% of the time, Pallas kernels for 0%

commit v1 on v0

--- a/solution.py
+++ b/solution.py
@@ -4,6 +4,24 @@
 from jax.sharding import PartitionSpec as P
 
 CAP = 32
+
+
+def collect(array, axis, dim):
+    ways, here, hop = (lax.axis_size(axis), lax.axis_index(axis), array.shape[dim])
+    dims = [n * ways if d == dim else n for d, n in enumerate(array.shape)]
+    full = lax.dynamic_update_slice_in_dim(
+        jnp.zeros(dims, array.dtype), array, here * hop, axis=dim
+    )
+    going_up = going_down = array
+    for far in range(1, ways // 2 + 1):
+        going_up = lax.ppermute(going_up, axis, [(d, (d + 1) % ways) for d in range(ways)])
+        full = lax.dynamic_update_slice_in_dim(full, going_up, (here - far) % ways * hop, axis=dim)
+        if 2 * far < ways:
+            going_down = lax.ppermute(going_down, axis, [(d, (d - 1) % ways) for d in range(ways)])
+            full = lax.dynamic_update_slice_in_dim(
+                full, going_down, (here + far) % ways * hop, axis=dim
+            )
+    return full
 
 
 def slot_layout(routes, num_experts):
@@ -48,7 +66,7 @@
         lax.psum_scatter(up_part, "pipe", scatter_dimension=3, tiled=True),
     )
     hidden_share = (jax.nn.silu(gate_share) * up_share).astype(jnp.bfloat16)
-    hidden = lax.all_gather(hidden_share, "pipe", axis=3, tiled=True)
+    hidden = collect(hidden_share, "pipe", 3)
     expert_out = jnp.einsum(
         "sjcf,jfd->sjcd", hidden, w_down, preferred_element_type=jnp.float32
     ).astype(jnp.bfloat16)

time: 396 us -> 355 us (0.90)
  waiting for transfers between devices: 262 us -> 207 us
  starting transfers between devices: 24.7 us -> 32.9 us
  local copies, waits for them, and re-layouts: 3.19 us -> 8.06 us
    all_gather x1 -> x0, waiting for transfers between devices: 40.6 us -> none  [local(): hidden = lax.all_gather(hidden_share, 'pipe', axis=3, tiled=True)]
    reduce_scatter x1, waiting for transfers between devices: 56.5 us -> 23 us  [local(): lax.psum_scatter(gate_part, 'pipe', scatter_dimension=3, tiled=True)]
    reduce_scatter x1, waiting for transfers between devices: 23 us -> 56.5 us  [local(): lax.psum_scatter(up_part, 'pipe', scatter_dimension=3, tiled=True)]
    all_gather x1, waiting for transfers between devices: 31.9 us -> 0.01 us  [local(): lax.all_gather(d_up_share, 'pipe', axis=3, tiled=True)]
    ppermute x0 -> x7, waiting for transfers between devices: none -> 28.4 us  [the longest x4 28.3 us: collect(): lax.ppermute(going_up, axis, [(d, (d + 1) % ways) for d in range(ways)])]
    all_gather x1, waiting for transfers between devices: 41.2 us -> 18.5 us  [local(): lax.all_gather(d_gate_share, 'pipe', axis=3, tiled=True)]
    all_to_all x1, waiting for transfers between devices: 0.01 us -> 12.8 us  [local(): lax.all_to_all(expert_out.reshape(num_experts, CAP, slice_width), ('dp',...]
    ppermute x0 -> x7, starting transfers between devices: none -> 10.6 us  [the longest x3 8.21 us: collect(): lax.ppermute(going_down, axis, [(d, (d - 1) % ways) for d in range(ways)])]
  transfers between devices with their start and end apart: 8 -> 14, of which waited for: 7 -> 10; matrix products, arithmetic and copies ran while one was open for 8% -> 9% of each run, Pallas kernels for 0% -> 0%
where the time goes in v1:
time: 355 us; the launch traced here: 354 us
  waiting for transfers between devices  207 us (58%)
  blocking collectives  46.1 us (13%)
  matrix products  40.2 us (11%)
  starting transfers between devices  32.9 us (9%)
  between operations  14.1 us (4%)
  local copies, waits for them, and re-layouts  8.06 us (2%)
  other arithmetic  5.83 us (2%)
    reduce_scatter x1, waiting for transfers between devices, local(): lax.psum_scatter(d_hidden_part, 'pipe', scatter_dimension=3, tiled=True)  56.6 us
    reduce_scatter x1, waiting for transfers between devices, local(): lax.psum_scatter(up_part, 'pipe', scatter_dimension=3, tiled=True)  56.5 us
    ppermute x4, waiting for transfers between devices, collect(): lax.ppermute(going_up, axis, [(d, (d + 1) % ways) for d in range(ways)])  28.3 us
    all_to_all x1, blocking collectives, local(): lax.all_to_all(outbound, ('dp', 'expert'), split_axis=0, concat_axis=0, t...  25.4 us
    reduce_scatter x1, waiting for transfers between devices, local(): lax.psum_scatter(gate_part, 'pipe', scatter_dimension=3, tiled=True)  23 us
    all_to_all x1, blocking collectives, local(): lax.all_to_all(scaled_out, ('dp', 'expert'), split_axis=0, concat_axis=0,...  20.7 us
    all_gather x1, waiting for transfers between devices, local(): lax.all_gather(d_gate_share, 'pipe', axis=3, tiled=True)  18.5 us
    all_to_all x1, waiting for transfers between devices, local(): lax.all_to_all(expert_out.reshape(num_experts, CAP, slice_width), ('dp',...  12.8 us
  transfers between devices with their start and end apart: 14, of which 10 were waited for; matrix products, arithmetic and copies ran while one was open for 9% of the time, Pallas kernels for 0%

profile of v1, /device:TPU:1, one launch (start us, length us, event | category | flops | bytes accessed | tf_op | source)
XLA Modules:
  0.0 353.9 jit_solution(17701921874020563196)
XLA Ops:
  7.2 0.0 reduce-scatter.4.cloned.1.call-start
  7.2 0.9 copy.64
  8.1 0.1 eq.52
  8.2 0.1 eq.48
  8.4 1.7 reduce-window.6
  10.1 0.3 slice_reduce_fusion
  10.4 0.1 fusion.37
  10.5 0.1 reduce_sum.30
  10.7 0.1 copy.67
  10.7 0.7 multiply_add_fusion
  11.5 0.4 convert_reduce_fusion
  11.8 1.3 convolution_convert_fusion
  13.2 25.4 %all_to_all.20 = bf16[32,32,512]{2,1,0:T(8,128)(2,1)S(1)} all-to-all(bf16[32,32,512]{2,1,0:T(8,128)(2,1)S(1)} %bitcast.118), channel_id=1, replica_groups=mesh['pipe'=8,'dp'=4,'expert'=8] {'dp','expert'}, dimensions={0} | all-to-all | bytes 2097152 | tf_op jit(solution)/shard_map/all_to_all | solution.py:55
  38.6 3.2 convolution_bitcast_fusion.2
  41.8 0.0 reduce-scatter.6.cloned.1.call-start
  41.9 4.5 %convolution_bitcast_fusion.1 = f32[32,1,32,1024]{3,2,0,1:T(8,128)} fusion(bf16[32,32,512]{2,1,0:T(8,128)(2,1)S(1)} %all_to_all.20, bf16[1,512,1024]{2,1,0:T(8,128)(2,1)} %param.11), kind=kOutput, calls=%fused_computation.4 | convolution fusion | flops 1073741824 | bytes 6291456 | tf_op jit(solution)/shard_map/sjcd,jdf->sjcf/dot_general | solution.py:63
  46.4 0.0 reduce-scatter.6.cloned.1.call-update
  46.4 0.0 reduce-scatter.8.cloned.1.call-start
  46.4 0.6 copy-done.6
  47.0 0.4 select_reduce_fusion
  47.4 1.0 convolution_convert_fusion.1
  48.4 20.7 %all_to_all.21 = bf16[32,32,512]{2,1,0:T(8,128)(2,1)S(1)} all-to-all(bf16[32,32,512]{2,1,0:T(8,128)(2,1)S(1)} %bitcast.119), channel_id=1, replica_groups=mesh['pipe'=8,'dp'=4,'expert'=8] {'dp','expert'}, dimensions={0} | all-to-all | bytes 2097152 | tf_op jit(solution)/shard_map/all_to_all | solution.py:56
  69.1 1.0 copy-done.1
  70.0 3.3 convolution_bitcast_fusion
  73.3 0.0 all-gather.5.cloned.1.call-start
  73.4 23.0 %reduce-scatter.4.cloned.1.call-done = f32[32,1,32,128]{3,2,0,1:T(8,128)} async-done(((f32[32,1,32,1024]{3,2,0,1:T(8,128)}), f32[32,1,32,128]{3,2,0,1:T(8,128)}) %reduce-scatter.4.cloned.1.call-update) | async-done | bytes 524304 | tf_op jit(solution)/shard_map/reduce_scatter | solution.py:65
  96.3 56.5 %reduce-scatter.6.cloned.1.call-done = f32[32,1,32,128]{3,2,0,1:T(8,128)} async-done(((f32[32,1,32,1024]{3,2,0,1:T(8,128)}), f32[32,1,32,128]{3,2,0,1:T(8,128)}) %reduce-scatter.6.cloned.1.call-update) | async-done | bytes 524304 | tf_op jit(solution)/shard_map/reduce_scatter | solution.py:66
  152.9 56.6 %reduce-scatter.8.cloned.1.call-done = f32[32,1,32,128]{3,2,0,1:T(8,128)} async-done(((f32[32,1,32,1024]{3,2,0,1:T(8,128)}), f32[32,1,32,128]{3,2,0,1:T(8,128)}) %reduce-scatter.8.cloned.1.call-update) | async-done | bytes 524304 | tf_op jit(solution)/shard_map/reduce_scatter | solution.py:83
  209.4 2.5 multiply_convert_fusion.1
  211.9 0.0 all-gather.5.cloned.1.call-update
  211.9 0.0 all-gather.3.cloned.1.call-start
  211.9 0.1 collective-permute-start
  212.2 2.5 collective-permute-start.1
  214.7 0.3 broadcast.40
  215.0 0.2 copy_dynamic-update-slice_fusion.7
  215.2 5.3 %collective-permute-done = bf16[32,1,32,128]{3,2,0,1:T(8,128)(2,1)} collective-permute-done((bf16[32,1,32,128]{3,2,0,1:T(8,128)(2,1)S(1)}, bf16[32,1,32,128]{3,2,0,1:T(8,128)(2,1)}, u32[]{:S(2)}, u32[]{:S(2)}) %collective-permute-start) | collective-permute-done | bytes 262176 | tf_op jit(solution)/shard_map/ppermute | solution.py:17
  220.5 1.1 copy_dynamic-update-slice_fusion.6
  221.6 2.8 collective-permute-start.3
  224.4 1.2 copy_dynamic-update-slice_fusion.5
  225.6 6.1 %collective-permute-done.2 = bf16[32,1,32,128]{3,2,0,1:T(8,128)(2,1)S(1)} collective-permute-done((bf16[32,1,32,128]{3,2,0,1:T(8,128)(2,1)}, bf16[32,1,32,128]{3,2,0,1:T(8,128)(2,1)S(1)}, u32[]{:S(2)}, u32[]{:S(2)}) %collective-permute-start.2) | collective-permute-done | bytes 262176 | tf_op jit(solution)/shard_map/ppermute | solution.py:17
  231.6 0.2 copy_dynamic-update-slice_fusion.4
  231.8 0.0 collective-permute-done.3
  231.8 2.9 collective-permute-start.5
  234.7 0.2 copy_dynamic-update-slice_fusion.3
  234.9 7.0 %collective-permute-done.4 = bf16[32,1,32,128]{3,2,0,1:T(8,128)(2,1)S(1)} collective-permute-done((bf16[32,1,32,128]{3,2,0,1:T(8,128)(2,1)S(1)}, bf16[32,1,32,128]{3,2,0,1:T(8,128)(2,1)S(1)}, u32[]{:S(2)}, u32[]{:S(2)}) %collective-permute-start.4) | collective-permute-done | bytes 262176 | tf_op jit(solution)/shard_map/ppermute | solution.py:17
  241.9 2.3 collective-permute-start.6
  244.3 0.2 copy_dynamic-update-slice_fusion.2
  244.4 0.2 copy_dynamic-update-slice_fusion.1
  244.6 9.9 %collective-permute-done.6 = bf16[32,1,32,128]{3,2,0,1:T(8,128)(2,1)S(1)} collective-permute-done((bf16[32,1,32,128]{3,2,0,1:T(8,128)(2,1)S(1)}, bf16[32,1,32,128]{3,2,0,1:T(8,128)(2,1)S(1)}, u32[]{:S(2)}, u32[]{:S(2)}) %collective-permute-start.6) | collective-permute-done | bytes 262176 | tf_op jit(solution)/shard_map/ppermute | solution.py:17
  254.5 0.2 copy_dynamic-update-slice_fusion
  254.7 1.3 copy-done.2
  256.1 2.4 fusion.16
  258.4 9.9 %all-to-all-start.1 = ((bf16[32,32,512]{2,1,0:T(8,128)(2,1)}), bf16[32,32,512]{2,1,0:T(8,128)(2,1)}, u32[]{:S(2)}, u32[]{:S(2)}) async-start(bf16[32,32,512]{2,1,0:T(8,128)(2,1)} %fusion.16), calls=%async_computation.3 | async-start | bytes 2097152 | tf_op jit(solution)/shard_map/all_to_all | solution.py:73
  268.4 4.3 %fusion.25 = bf16[1,1024,512]{2,1,0:T(8,128)(2,1)} fusion(bf16[32,32,1024]{2,0,1:T(8,128)(2,1)} %copy-done.2, bf16[32,32,512]{2,1,0:T(8,128)(2,1)} %copy-done.1), kind=kOutput, calls=%fused_computation.25 | convolution fusion | flops 1074266112 | bytes 4194304 | tf_op jit(solution)/shard_map/sjcf,sjcd->jfd/dot_general | solution.py:115
  272.6 12.8 %all-to-all-done.1 = bf16[32,32,512]{2,1,0:T(8,128)(2,1)} async-done(((bf16[32,32,512]{2,1,0:T(8,128)(2,1)}), bf16[32,32,512]{2,1,0:T(8,128)(2,1)}, u32[]{:S(2)}, u32[]{:S(2)}) %all-to-all-start.1) | async-done | bytes 1048608 | tf_op jit(solution)/shard_map/all_to_all | solution.py:73
  285.5 2.6 convolution_convert_fusion.3
  288.0 4.5 %fusion.2 = f32[32,32,512]{2,1,0:T(8,128)} fusion(bf16[32,1,32,1024]{3,2,0,1:T(8,128)(2,1)} %all-gather.5.cloned.1.call-done, bf16[1,512,1024]{2,1,0:T(8,128)(2,1)} %param.11), kind=kOutput, calls=%fused_computation.11 | convolution fusion | flops 1073741824 | bytes 5242880 | tf_op jit(solution)/shard_map/sjcf,jdf->sjcd/dot_general | solution.py:95
  292.5 18.5 %all-gather.3.cloned.1.call-done = bf16[32,1,32,1024]{3,2,0,1:T(8,128)(2,1)} async-done(((bf16[32,1,32,128]{3,2,0,1:T(8,128)(2,1)}), bf16[32,1,32,1024]{3,2,0,1:T(8,128)(2,1)}) %all-gather.3.cloned.1.call-update) | async-done | bytes 2097168 | tf_op jit(solution)/shard_map/all_gather | solution.py:90
  311.0 4.8 %add_convert_fusion = bf16[32,32,512]{2,1,0:T(8,128)(2,1)} fusion(f32[32,32,512]{2,1,0:T(8,128)} %fusion.2, bf16[32,1,32,1024]{3,2,0,1:T(8,128)(2,1)} %all-gather.3.cloned.1.call-done, bf16[1,512,1024]{2,1,0:T(8,128)(2,1)} %param.10), kind=kOutput, calls=%fused_computation.19 | convolution fusion | flops 1074790400 | bytes 6291456 | tf_op jit(solution)/shard_map/sjcf,jdf->sjcd/dot_general | solution.py:94
  315.8 12.2 %all-to-all-start.3 = ((bf16[32,32,512]{2,1,0:T(8,128)(2,1)}), bf16[32,32,512]{2,1,0:T(8,128)(2,1)}, u32[]{:S(2)}, u32[]{:S(2)}) async-start(bf16[32,32,512]{2,1,0:T(8,128)(2,1)} %add_convert_fusion), calls=%async_computation.6 | async-start | bytes 2097152 | tf_op jit(solution)/shard_map/all_to_all | solution.py:97
  328.0 4.0 %fusion.19 = bf16[1,512,1024]{2,1,0:T(8,128)(2,1)} fusion(bf16[32,32,512]{2,1,0:T(8,128)(2,1)S(1)} %all_to_all.20, bf16[32,1,32,1024]{3,2,0,1:T(8,128)(2,1)} %all-gather.3.cloned.1.call-done), kind=kOutput, calls=%fused_computation.23 | convolution fusion | flops 1074266112 | bytes 4194304 | tf_op jit(solution)/shard_map/sjcd,sjcf->jdf/dot_general | solution.py:109
  332.0 2.3 fusion.22
  334.3 10.8 %all-to-all-done.3 = bf16[32,32,512]{2,1,0:T(8,128)(2,1)} async-done(((bf16[32,32,512]{2,1,0:T(8,128)(2,1)}), bf16[32,32,512]{2,1,0:T(8,128)(2,1)}, u32[]{:S(2)}, u32[]{:S(2)}) %all-to-all-start.3) | async-done | bytes 1048608 | tf_op jit(solution)/shard_map/all_to_all | solution.py:97
  345.1 2.2 convolution_convert_fusion.2
  (21 shorter events, 0.1 us)
Async XLA Ops:
  7.2 62.9 %copy-start = (bf16[1,1024,512]{2,1,0:T(8,128)(2,1)S(1)}, bf16[1,1024,512]{2,1,0:T(8,128)(2,1)}, u32[]{:S(2)}) copy-start(bf16[1,1024,512]{2,1,0:T(8,128)(2,1)} %param.12) | copy-start | bytes 3145732
  7.2 89.1 %reduce-scatter.4.cloned.1.call-start = ((), (), s32[]{:S(2)}) async-start(), calls=%async_computation.7 | async-start | bytes 4718592 | tf_op jit(solution)/shard_map/reduce_scatter | solution.py:65
  11.5 27.1 %copy-start.4 = (bf16[1,512,1024]{2,1,0:T(8,128)(2,1)S(1)}, bf16[1,512,1024]{2,1,0:T(8,128)(2,1)}, u32[]{:S(2)}) copy-start(bf16[1,512,1024]{2,1,0:T(8,128)(2,1)} %param.10) | copy-start | bytes 3145732
  41.8 111.0 %reduce-scatter.6.cloned.1.call-start = ((), (), s32[]{:S(2)}) async-start(), calls=%async_computation.8 | async-start | bytes 4718592 | tf_op jit(solution)/shard_map/reduce_scatter | solution.py:66
  46.4 0.7 copy-start.6
  46.4 1.1 copy-start.5
  46.4 163.0 %reduce-scatter.8.cloned.1.call-start = ((), (), s32[]{:S(2)}) async-start(), calls=%async_computation.9 | async-start | bytes 4718592 | tf_op jit(solution)/shard_map/reduce_scatter | solution.py:83
  69.1 1.0 copy-start.1
  73.3 214.7 %all-gather.5.cloned.1.call-start = ((), (), s32[]{:S(2)}) async-start(), calls=%async_computation.11 | async-start | bytes 2359296 | tf_op jit(solution)/shard_map/all_gather | solution.py:91
  211.9 99.1 %all-gather.3.cloned.1.call-start = ((), (), s32[]{:S(2)}) async-start(), calls=%async_computation.10 | async-start | bytes 2359296 | tf_op jit(solution)/shard_map/all_gather | solution.py:90
  211.9 8.5 %collective-permute-start = (bf16[32,1,32,128]{3,2,0,1:T(8,128)(2,1)S(1)}, bf16[32,1,32,128]{3,2,0,1:T(8,128)(2,1)}, u32[]{:S(2)}, u32[]{:S(2)}) collective-permute-start(bf16[32,1,32,128]{3,2,0,1:T(8,128)(2,1)S(1)} %get-tuple-element.6), channel_id=1, source_target_pairs={{0,32},{32,64},{64,96},{96,128},{128,160},{160,192},{192,224},{224... | collective-permute-start | bytes 786440 | tf_op jit(solution)/shard_map/ppermute | solution.py:17
  212.2 9.5 %collective-permute-start.1 = (bf16[32,1,32,128]{3,2,0,1:T(8,128)(2,1)S(1)}, bf16[32,1,32,128]{3,2,0,1:T(8,128)(2,1)}, u32[]{:S(2)}, u32[]{:S(2)}) collective-permute-start(bf16[32,1,32,128]{3,2,0,1:T(8,128)(2,1)S(1)} %get-tuple-element.6), channel_id=1, source_target_pairs={{0,224},{32,0},{64,32},{96,64},{128,96},{160,128},{192,160},{224,1... | collective-permute-start | bytes 786440 | tf_op jit(solution)/shard_map/ppermute | solution.py:20
  220.5 11.1 %collective-permute-start.2 = (bf16[32,1,32,128]{3,2,0,1:T(8,128)(2,1)}, bf16[32,1,32,128]{3,2,0,1:T(8,128)(2,1)S(1)}, u32[]{:S(2)}, u32[]{:S(2)}) collective-permute-start(bf16[32,1,32,128]{3,2,0,1:T(8,128)(2,1)} %collective-permute-done), channel_id=1, source_target_pairs={{0,32},{32,64},{64,96},{96,128},{128,160},{160,192},{192,224},{224... | collective-permute-start | bytes 786440 | tf_op jit(solution)/shard_map/ppermute | solution.py:17
  221.6 10.2 %collective-permute-start.3 = (bf16[32,1,32,128]{3,2,0,1:T(8,128)(2,1)}, bf16[32,1,32,128]{3,2,0,1:T(8,128)(2,1)S(1)}, u32[]{:S(2)}, u32[]{:S(2)}) collective-permute-start(bf16[32,1,32,128]{3,2,0,1:T(8,128)(2,1)} %collective-permute-done.1), channel_id=1, source_target_pairs={{0,224},{32,0},{64,32},{96,64},{128,96},{160,128},{192,160},{224,1... | collective-permute-start | bytes 786440 | tf_op jit(solution)/shard_map/ppermute | solution.py:20
  231.6 10.3 %collective-permute-start.4 = (bf16[32,1,32,128]{3,2,0,1:T(8,128)(2,1)S(1)}, bf16[32,1,32,128]{3,2,0,1:T(8,128)(2,1)S(1)}, u32[]{:S(2)}, u32[]{:S(2)}) collective-permute-start(bf16[32,1,32,128]{3,2,0,1:T(8,128)(2,1)S(1)} %collective-permute-done.2), channel_id=1, source_target_pairs={{0,32},{32,64},{64,96},{96,128},{128,160},{160,192},{192,224},{224... | collective-permute-start | bytes 786440 | tf_op jit(solution)/shard_map/ppermute | solution.py:17
  231.8 12.6 %collective-permute-start.5 = (bf16[32,1,32,128]{3,2,0,1:T(8,128)(2,1)S(1)}, bf16[32,1,32,128]{3,2,0,1:T(8,128)(2,1)S(1)}, u32[]{:S(2)}, u32[]{:S(2)}) collective-permute-start(bf16[32,1,32,128]{3,2,0,1:T(8,128)(2,1)S(1)} %collective-permute-done.3), channel_id=1, source_target_pairs={{0,224},{32,0},{64,32},{96,64},{128,96},{160,128},{192,160},{224,1... | collective-permute-start | bytes 786440 | tf_op jit(solution)/shard_map/ppermute | solution.py:20
  241.9 12.6 %collective-permute-start.6 = (bf16[32,1,32,128]{3,2,0,1:T(8,128)(2,1)S(1)}, bf16[32,1,32,128]{3,2,0,1:T(8,128)(2,1)S(1)}, u32[]{:S(2)}, u32[]{:S(2)}) collective-permute-start(bf16[32,1,32,128]{3,2,0,1:T(8,128)(2,1)S(1)} %collective-permute-done.4), channel_id=1, source_target_pairs={{0,32},{32,64},{64,96},{96,128},{128,160},{160,192},{192,224},{224... | collective-permute-start | bytes 786440 | tf_op jit(solution)/shard_map/ppermute | solution.py:17
  254.7 1.3 copy-start.2
  258.4 27.1 %all-to-all-start.1 = ((bf16[32,32,512]{2,1,0:T(8,128)(2,1)}), bf16[32,32,512]{2,1,0:T(8,128)(2,1)}, u32[]{:S(2)}, u32[]{:S(2)}) async-start(bf16[32,32,512]{2,1,0:T(8,128)(2,1)} %fusion.16), calls=%async_computation.3 | async-start | bytes 2097152 | tf_op jit(solution)/shard_map/all_to_all | solution.py:73
  315.8 29.3 %all-to-all-start.3 = ((bf16[32,32,512]{2,1,0:T(8,128)(2,1)}), bf16[32,32,512]{2,1,0:T(8,128)(2,1)}, u32[]{:S(2)}, u32[]{:S(2)}) async-start(bf16[32,32,512]{2,1,0:T(8,128)(2,1)} %add_convert_fusion), calls=%async_computation.6 | async-start | bytes 2097152 | tf_op jit(solution)/shard_map/all_to_all | solution.py:97
  328.0 4.0 %copy-start.3 = (bf16[32,1,32,1024]{3,2,0,1:T(8,128)(2,1)S(1)}, bf16[32,1,32,1024]{3,2,0,1:T(8,128)(2,1)}, u32[]{:S(2)}) copy-start(bf16[32,1,32,1024]{3,2,0,1:T(8,128)(2,1)} %all-gather.5.cloned.1.call-done) | copy-start | bytes 6291460
Sparse Core Ops, SparseCore 0:
  42.0 54.3 reduce-scatter.3
  98.9 53.9 reduce-scatter.5
  155.4 53.9 reduce-scatter.7
  212.0 51.5 all-gather.4
  265.2 45.7 all-gather.2
